TPU v7x, 256 devices: a whole 4x4x8 slice. The times are simulated.
256 devices in a mesh: space: 32 (over x, y, core), tm: 8 (over z).
Axes of the slice: x: 4, y: 4, z: 8, core: 2. Of those that a mesh axis runs over, the one named last changes fastest.
Arguments:
- velocity: bfloat16 [256, 2, 512, 1024], P('tm', None, 'space'), may hold values from -8.4 to 8.4
Outputs:
- vorticity: bfloat16 [256, 512, 1024], P('tm', 'space')
- modes: float32 [32, 512, 1024], P('tm', 'space')
All inputs are finite; a program needn't handle non-finite values.
Results may differ from a plain program's by a relative error of at most 0.003.
Values may be sent and summed in bfloat16 or wider, within the bound.
A program may use at most 64 MiB of HBM per device.

v0:
```python
import jax
import jax.numpy as jnp
from jax import lax
from jax.sharding import PartitionSpec as P

RANK = 32
HIGH = lax.Precision.HIGHEST


def halo_rows(block, width):
    count = lax.axis_size("space")
    forward = [(i, (i + 1) % count) for i in range(count)]
    backward = [(target, source) for source, target in forward]
    rows = block.shape[1]
    low = lax.ppermute(block[:, rows - width :], "space", forward)
    high = lax.ppermute(block[:, :width], "space", backward)
    return jnp.concatenate([low, block, high], axis=1)


def spanwise(field):
    ahead = jnp.roll(field, -1, 2)
    behind = jnp.roll(field, 1, 2)
    ahead_two = jnp.roll(field, -2, 2)
    behind_two = jnp.roll(field, 2, 2)
    return (8.0 * (ahead - behind) - (ahead_two - behind_two)) / 12.0


def merge_small(gram):
    coeffs = gram[:, :, :RANK] + gram[:, :, RANK:]
    diagonal = jnp.diagonal(gram, axis1=1, axis2=2)
    scales = jnp.sqrt(diagonal[:, :RANK] + diagonal[:, RANK:])
    half = jnp.einsum("nab,nbc->nac", gram, coeffs, precision=HIGH)
    inner = jnp.einsum("nab,nac->nbc", coeffs, half, precision=HIGH)
    lower = jnp.linalg.cholesky(inner)
    eye = jnp.broadcast_to(jnp.eye(RANK, dtype=jnp.float32), inner.shape)
    lower_inv = lax.linalg.triangular_solve(lower, eye, left_side=True, lower=True)
    factor = jnp.swapaxes(lower_inv, 1, 2) * scales[:, None, :]
    return jnp.einsum("nab,nbc->nac", coeffs, factor, precision=HIGH)


def tree_basis(gram, leaves):
    width = leaves * RANK
    basis = None
    span = 1
    while span < leaves:
        nodes = leaves // (2 * span)
        size = 2 * span * RANK
        sub = jnp.stack(
            [gram[k * size : (k + 1) * size, k * size : (k + 1) * size] for k in range(nodes)]
        )
        if basis is None:
            h = sub
        else:
            b = basis.reshape(nodes, 2, span * RANK, RANK)
            zero = jnp.zeros_like(b[:, 0])
            bd = jnp.concatenate(
                [
                    jnp.concatenate([b[:, 0], zero], axis=2),
                    jnp.concatenate([zero, b[:, 1]], axis=2),
                ],
                axis=1,
            )
            gb = jnp.einsum("nab,nbc->nac", sub, bd, precision=HIGH)
            h = jnp.einsum("nab,nac->nbc", bd, gb, precision=HIGH)
        c = merge_small(h)
        if basis is None:
            basis = c
        else:
            basis = jnp.einsum("nab,nbc->nac", bd, c, precision=HIGH)
        span *= 2
    return basis.reshape(width, RANK)


def local(velocity):
    rows = velocity.shape[2]
    span_v = halo_rows(velocity[:, 1], 2).astype(jnp.float32)
    stream_u = velocity[:, 0].astype(jnp.float32)
    dv_dx = (
        8.0 * (span_v[:, 3 : rows + 3] - span_v[:, 1 : rows + 1])
        - (span_v[:, 4:] - span_v[:, :rows])
    ) / 12.0
    vorticity = (dv_dx - spanwise(stream_u)).astype(jnp.bfloat16)
    blocks = lax.axis_size("tm")
    cells = lax.all_to_all(vorticity, "tm", 2, 0, tiled=True)
    flat = cells.reshape(cells.shape[0], -1)
    gram = jnp.einsum("ax,bx->ab", flat, flat, preferred_element_type=jnp.float32)
    gram = lax.psum(gram, ("space", "tm"))
    basis = tree_basis(gram, blocks)
    part = jnp.einsum("ab,ax->bx", basis, flat.astype(jnp.float32), precision=HIGH).reshape(
        RANK, rows, -1
    )
    modes = lax.all_to_all(part, "tm", 0, 2, tiled=True)
    return (vorticity, modes)


def solution(mesh):
    in_specs = (P("tm", None, "space", None),)
    out_specs = (P("tm", "space", None), P("tm", "space", None))
    return jax.shard_map(local, mesh=mesh, in_specs=in_specs, out_specs=out_specs, check_vma=False)
```

profile of v0, /device:TPU:2, one launch (start us, length us, event | category | flops | bytes accessed | tf_op | source)
XLA Modules:
  0.0 411.2 jit_solution(9131504356403751906)
XLA Ops:
  7.2 1.9 bitcast_convert_fusion
  9.7 3.8 collective-permute-start.1
  15.4 0.8 collective-permute-done
  17.2 2.2 fusion.3
  19.4 5.1 %copy.130 = bf16[32,16,1024]{0,1,2:T(8,128)(2,1)} copy(bf16[32,16,1024]{2,1,0:T(8,128)(2,1)S(1)} %fusion.3) | data formatting | bytes 2097152 | tf_op jit(solution)/shard_map/convert_element_type | solution.py:82
  24.5 7.8 %reshape.157 = bf16[8,2,32768]{2,1,0:T(2,128)(2,1)} reshape(bf16[1024,16,32]{2,1,0:T(8,128)(2,1)} %bitcast.133) | data formatting | bytes 2097152
  32.4 8.5 %all-to-all-start = ((bf16[8,2,32768]{2,1,0:T(2,128)(2,1)}), bf16[8,2,32768]{2,1,0:T(2,128)(2,1)S(1)}, u32[]{:S(2)}, u32[]{:S(2)}) async-start(bf16[8,2,32768]{2,1,0:T(2,128)(2,1)} %reshape.157), calls=%async_computation | async-start | bytes 2097152 | tf_op jit(solution)/shard_map/all_to_all | solution.py:84
  41.1 28.5 %all-to-all-done = bf16[8,2,32768]{2,1,0:T(2,128)(2,1)S(1)} async-done(((bf16[8,2,32768]{2,1,0:T(2,128)(2,1)}), bf16[8,2,32768]{2,1,0:T(2,128)(2,1)S(1)}, u32[]{:S(2)}, u32[]{:S(2)}) %all-to-all-start) | async-done | bytes 1048608 | tf_op jit(solution)/shard_map/all_to_all | solution.py:84
  69.6 4.5 %reshape.158 = bf16[1024,16,32]{2,1,0:T(8,128)(2,1)} reshape(bf16[8,2,32768]{2,1,0:T(2,128)(2,1)S(1)} %all-to-all-done) | data formatting | bytes 2097152
  74.1 5.4 %copy.131 = bf16[32,16,8,128]{3,1,0,2:T(8,128)(2,1)S(1)} copy(bf16[32,16,8,128]{0,1,3,2:T(8,128)(2,1)} %bitcast.132) | data formatting | bytes 2097152 | tf_op jit(solution)/shard_map/all_to_all | solution.py:84
  79.5 1.2 fusion.10
  82.2 244.6 %all-reduce.6.cloned.1.call-done = f32[256,256]{0,1:T(8,128)} async-done(((f32[256,256]{0,1:T(8,128)}), f32[256,256]{0,1:T(8,128)}) %all-reduce.6.cloned.1.call-update) | async-done | bytes 262160 | tf_op jit(solution)/shard_map/psum | solution.py:87
  326.8 0.9 slice_bitcast_fusion.7
  327.8 1.9 copy.137
  329.7 0.9 fusion.70
  330.6 1.5 gather_fusion
  332.0 0.8 copy.138
  332.9 1.1 fusion.69
  334.1 11.7 %custom-call.21 = f32[4,32,32]{2,1,0:T(8,128)S(1)} custom-call(f32[4,32,32]{2,1,0:T(8,128)S(1)} %fusion.19), custom_call_target="Cholesky" | custom-call | tf_op jit(solution)/shard_map/jit(cholesky)/cholesky | solution.py:34
  346.1 9.8 %custom-call.22 = f32[4,1,32,32]{2,3,1,0:T(8,128)S(1)} custom-call(f32[4,1,32,32]{3,2,1,0:T(8,128)S(1)} %select_bitcast_fusion), custom_call_target="InvertDiagBlocksLowerTriangular" | custom-call | tf_op jit(solution)/shard_map/triangular_solve | solution.py:36
  355.9 0.9 convolution_multiply_fusion
  357.8 1.9 copy.147
  360.5 1.5 gather_fusion.1
  362.0 0.8 copy.148
  362.9 0.9 fusion.66
  363.9 5.9 %custom-call.23 = f32[2,32,32]{2,1,0:T(8,128)S(1)} custom-call(f32[2,32,32]{2,1,0:T(8,128)S(1)} %fusion.32), custom_call_target="Cholesky" | custom-call | tf_op jit(solution)/shard_map/jit(cholesky)/cholesky | solution.py:34
  370.0 4.9 %custom-call.24 = f32[2,1,32,32]{2,3,1,0:T(8,128)S(1)} custom-call(f32[2,1,32,32]{3,2,1,0:T(8,128)S(1)} %select_bitcast_fusion.1), custom_call_target="InvertDiagBlocksLowerTriangular" | custom-call | tf_op jit(solution)/shard_map/triangular_solve | solution.py:36
  375.0 0.9 convolution_multiply_fusion.1
  378.1 2.9 custom-call.25
  382.3 2.4 custom-call.26
  385.4 1.0 fusion.76
  386.6 17.1 %all_to_all.33 = f32[32,16,128]{2,1,0:T(8,128)S(1)} all-to-all(f32[32,16,128]{2,1,0:T(8,128)S(1)} %copy.153), channel_id=1, replica_groups=mesh['space'=32,'tm'=8] {'tm'}, dimensions={0} | all-to-all | bytes 524288 | tf_op jit(solution)/shard_map/all_to_all | solution.py:92
  (61 shorter events, 12.6 us)
Async XLA Ops:
  9.6 6.6 %collective-permute-start = (bf16[32,2,1024]{2,0,1:T(8,128)(2,1)S(1)}, bf16[32,2,1024]{2,0,1:T(8,128)(2,1)S(1)}, u32[]{:S(2)}, u32[]{:S(2)}) collective-permute-start(bf16[32,2,1024]{2,0,1:T(8,128)(2,1)S(1)} %get-tuple-element.18), channel_id=1, source_target_pairs={{0,8},{8,16},{16,24},{24,32},{32,40},{40,48},{48,56},{56,64},{64,7... | collective-permute-start | bytes 393224 | tf_op jit(solution)/shard_map/ppermute | solution.py:15
  9.7 6.5 %collective-permute-start.1 = (bf16[32,2,1024]{2,0,1:T(8,128)(2,1)S(1)}, bf16[32,2,1024]{2,0,1:T(8,128)(2,1)S(1)}, u32[]{:S(2)}, u32[]{:S(2)}) collective-permute-start(bf16[32,2,1024]{2,0,1:T(8,128)(2,1)S(1)} %get-tuple-element.19), channel_id=1, source_target_pairs={{8,0},{16,8},{24,16},{32,24},{40,32},{48,40},{56,48},{64,56},{72,6... | collective-permute-start | bytes 393224 | tf_op jit(solution)/shard_map/ppermute | solution.py:16
  19.4 5.1 %copy-start = (bf16[32,16,1024]{2,1,0:T(8,128)(2,1)}, bf16[32,16,1024]{2,1,0:T(8,128)(2,1)S(1)}, u32[]{:S(2)}) copy-start(bf16[32,16,1024]{2,1,0:T(8,128)(2,1)S(1)} %fusion.3) | copy-start | bytes 3145732
  32.4 37.2 %all-to-all-start = ((bf16[8,2,32768]{2,1,0:T(2,128)(2,1)}), bf16[8,2,32768]{2,1,0:T(2,128)(2,1)S(1)}, u32[]{:S(2)}, u32[]{:S(2)}) async-start(bf16[8,2,32768]{2,1,0:T(2,128)(2,1)} %reshape.157), calls=%async_computation | async-start | bytes 2097152 | tf_op jit(solution)/shard_map/all_to_all | solution.py:84
  40.8 286.0 %all-reduce.6.cloned.1.call-start = ((), (), s32[]{:S(2)}) async-start(), calls=%async_computation.2 | async-start | bytes 524288 | tf_op jit(solution)/shard_map/psum | solution.py:87
  327.7 29.5 %copy-start.1 = (f32[256,256]{0,1:T(8,128)S(1)}, f32[256,256]{0,1:T(8,128)}, u32[]{:S(2)}) copy-start(f32[256,256]{0,1:T(8,128)} %all-reduce.6.cloned.1.call-done) | copy-start | bytes 786436
Sparse Core Ops, SparseCore 0:
  80.8 245.9 all-reduce.5
where the time goes:
time: 412 us; the launch traced here: 411 us
  waiting for transfers between devices  274 us (67%)
  other arithmetic  44.8 us (11%)
  local copies, waits for them, and re-layouts  37.9 us (9%)
  blocking collectives  17.1 us (4%)
  between operations  14.4 us (3%)
  starting transfers between devices  12.6 us (3%)
  matrix products  10.4 us (3%)
    psum x1, waiting for transfers between devices, local(): gram = lax.psum(gram, ('space', 'tm'))  245 us
    all_to_all x1, waiting for transfers between devices, local(): cells = lax.all_to_all(vorticity, 'tm', 2, 0, tiled=True)  28.5 us
    another operation x9, other arithmetic, merge_small(): lower = jnp.linalg.cholesky(inner)  21.5 us
    another operation x7, other arithmetic, merge_small(): lax.linalg.triangular_solve(lower, eye, left_side=True, lower=True)  18 us
    all_to_all x1, blocking collectives, local(): modes = lax.all_to_all(part, 'tm', 0, 2, tiled=True)  17.1 us
    unnamed x8, local copies, waits for them, and re-layouts  13.2 us
    all_to_all x1, starting transfers between devices, local(): cells = lax.all_to_all(vorticity, 'tm', 2, 0, tiled=True)  8.47 us
  transfers between devices with their start and end apart: 4, of which 3 were waited for; matrix products, arithmetic and copies ran while one was open for 1% of the time, Pallas kernels for 0%

commit v1 on v0

--- a/solution.py
+++ b/solution.py
@@ -5,6 +5,11 @@
 
 RANK = 32
 HIGH = lax.Precision.HIGHEST
+
+
+def one_after_other(value, axis_one, axis_two):
+    partial = lax.psum(value, axis_one)
+    return lax.psum(partial, axis_two)
 
 
 def halo_rows(block, width):
@@ -84,7 +89,7 @@
     cells = lax.all_to_all(vorticity, "tm", 2, 0, tiled=True)
     flat = cells.reshape(cells.shape[0], -1)
     gram = jnp.einsum("ax,bx->ab", flat, flat, preferred_element_type=jnp.float32)
-    gram = lax.psum(gram, ("space", "tm"))
+    gram = one_after_other(gram, "tm", "space")
     basis = tree_basis(gram, blocks)
     part = jnp.einsum("ab,ax->bx", basis, flat.astype(jnp.float32), precision=HIGH).reshape(
         RANK, rows, -1

time: 412 us -> 348 us (0.84)
  waiting for transfers between devices: 274 us -> 180 us
  blocking collectives: 17.1 us -> 56 us
  starting transfers between devices: 12.6 us -> 4.18 us
    psum x1 -> x2, waiting for transfers between devices: 245 us -> 179 us  [the longest x1 111 us: one_after_other(): return lax.psum(partial, axis_two)]
    all_to_all x0 -> x1, blocking collectives: none -> 37 us  [local(): cells = lax.all_to_all(vorticity, 'tm', 2, 0, tiled=True)]
    all_to_all x1 -> x0, waiting for transfers between devices: 28.5 us -> none  [local(): cells = lax.all_to_all(vorticity, 'tm', 2, 0, tiled=True)]
    all_to_all x1 -> x0, starting transfers between devices: 8.47 us -> none  [local(): cells = lax.all_to_all(vorticity, 'tm', 2, 0, tiled=True)]
where the time goes in v1:
time: 348 us; the launch traced here: 347 us
  waiting for transfers between devices  180 us (52%)
  blocking collectives  56 us (16%)
  other arithmetic  44.8 us (13%)
  local copies, waits for them, and re-layouts  37.1 us (11%)
  between operations  14.4 us (4%)
  matrix products  10.4 us (3%)
  starting transfers between devices  4.18 us (1%)
    psum x1, waiting for transfers between devices, one_after_other(): return lax.psum(partial, axis_two)  111 us
    psum x1, waiting for transfers between devices, one_after_other(): partial = lax.psum(value, axis_one)  68 us
    all_to_all x1, blocking collectives, local(): cells = lax.all_to_all(vorticity, 'tm', 2, 0, tiled=True)  37 us
    another operation x9, other arithmetic, merge_small(): lower = jnp.linalg.cholesky(inner)  21.5 us
    all_to_all x1, blocking collectives, local(): modes = lax.all_to_all(part, 'tm', 0, 2, tiled=True)  19 us
    another operation x7, other arithmetic, merge_small(): lax.linalg.triangular_solve(lower, eye, left_side=True, lower=True)  18 us
    unnamed x8, local copies, waits for them, and re-layouts  12.4 us
  transfers between devices with their start and end apart: 4, of which 3 were waited for; matrix products, arithmetic and copies ran while one was open for 1% of the time, Pallas kernels for 0%

profile of v1, /device:TPU:2, one launch (start us, length us, event | category | flops | bytes accessed | tf_op | source)
XLA Modules:
  0.0 347.1 jit_solution(7667016777236550402)
XLA Ops:
  7.2 1.9 bitcast_convert_fusion
  9.8 3.8 %collective-permute-start.1 = (bf16[32,2,1024]{2,0,1:T(8,128)(2,1)S(1)}, bf16[32,2,1024]{2,0,1:T(8,128)(2,1)S(1)}, u32[]{:S(2)}, u32[]{:S(2)}) collective-permute-start(bf16[32,2,1024]{2,0,1:T(8,128)(2,1)S(1)} %get-tuple-element.19), channel_id=1, source_target_pairs={{8,0},{16,8},{24,16},{32,24},{40,32},{48,40},{56,48},{64,56},{72,6... | collective-permute-start | bytes 393224 | tf_op jit(solution)/shard_map/ppermute | solution.py:21
  15.4 0.8 collective-permute-done
  17.2 2.2 fusion.3
  19.5 5.1 %copy.130 = bf16[32,16,1024]{0,1,2:T(8,128)(2,1)} copy(bf16[32,16,1024]{2,1,0:T(8,128)(2,1)S(1)} %fusion.3) | data formatting | bytes 2097152 | tf_op jit(solution)/shard_map/convert_element_type | solution.py:87
  24.6 7.0 %reshape.157 = bf16[8,2,32768]{2,1,0:T(2,128)(2,1)S(1)} reshape(bf16[1024,16,32]{2,1,0:T(8,128)(2,1)} %bitcast.133) | data formatting | bytes 2097152
  31.6 37.0 %all_to_all.33 = bf16[8,2,32768]{2,1,0:T(2,128)(2,1)S(1)} all-to-all(bf16[8,2,32768]{2,1,0:T(2,128)(2,1)S(1)} %reshape.157), channel_id=1, replica_groups=mesh['space'=32,'tm'=8] {'tm'}, dimensions={0} | all-to-all | bytes 2097152 | tf_op jit(solution)/shard_map/all_to_all | solution.py:89
  68.6 4.5 %reshape.158 = bf16[1024,16,32]{2,1,0:T(8,128)(2,1)} reshape(bf16[8,2,32768]{2,1,0:T(2,128)(2,1)S(1)} %all_to_all.33) | data formatting | bytes 2097152
  73.1 5.4 %copy.131 = bf16[32,16,8,128]{3,1,0,2:T(8,128)(2,1)S(1)} copy(bf16[32,16,8,128]{0,1,3,2:T(8,128)(2,1)} %bitcast.132) | data formatting | bytes 2097152 | tf_op jit(solution)/shard_map/all_to_all | solution.py:89
  78.5 1.2 fusion.10
  80.0 68.0 %all-reduce.7.cloned.1.call-done = f32[256,256]{0,1:T(8,128)} async-done(((f32[256,256]{0,1:T(8,128)}), f32[256,256]{0,1:T(8,128)}) %all-reduce.7.cloned.1.call-update) | async-done | bytes 262160 | tf_op jit(solution)/shard_map/psum | solution.py:11
  149.4 111.4 %all-reduce.9.cloned.1.call-done = f32[256,256]{0,1:T(8,128)} async-done(((f32[256,256]{0,1:T(8,128)}), f32[256,256]{0,1:T(8,128)}) %all-reduce.9.cloned.1.call-update) | async-done | bytes 262160 | tf_op jit(solution)/shard_map/psum | solution.py:12
  260.8 0.9 slice_bitcast_fusion.7
  261.7 1.9 copy.137
  263.7 0.9 fusion.70
  264.5 1.5 gather_fusion
  266.0 0.8 copy.138
  266.9 1.1 fusion.69
  268.1 11.7 %custom-call.21 = f32[4,32,32]{2,1,0:T(8,128)S(1)} custom-call(f32[4,32,32]{2,1,0:T(8,128)S(1)} %fusion.19), custom_call_target="Cholesky" | custom-call | tf_op jit(solution)/shard_map/jit(cholesky)/cholesky | solution.py:39
  280.1 9.8 %custom-call.22 = f32[4,1,32,32]{2,3,1,0:T(8,128)S(1)} custom-call(f32[4,1,32,32]{3,2,1,0:T(8,128)S(1)} %select_bitcast_fusion), custom_call_target="InvertDiagBlocksLowerTriangular" | custom-call | tf_op jit(solution)/shard_map/triangular_solve | solution.py:41
  289.9 0.9 convolution_multiply_fusion
  291.8 1.9 copy.147
  294.5 1.5 gather_fusion.1
  296.0 0.8 copy.148
  296.9 0.9 fusion.66
  297.9 5.9 %custom-call.23 = f32[2,32,32]{2,1,0:T(8,128)S(1)} custom-call(f32[2,32,32]{2,1,0:T(8,128)S(1)} %fusion.32), custom_call_target="Cholesky" | custom-call | tf_op jit(solution)/shard_map/jit(cholesky)/cholesky | solution.py:39
  304.0 4.9 %custom-call.24 = f32[2,1,32,32]{2,3,1,0:T(8,128)S(1)} custom-call(f32[2,1,32,32]{3,2,1,0:T(8,128)S(1)} %select_bitcast_fusion.1), custom_call_target="InvertDiagBlocksLowerTriangular" | custom-call | tf_op jit(solution)/shard_map/triangular_solve | solution.py:41
  308.9 0.9 convolution_multiply_fusion.1
  312.0 2.9 custom-call.25
  316.3 2.4 custom-call.26
  319.4 1.0 fusion.76
  320.5 19.0 %all_to_all.34 = f32[32,16,128]{2,1,0:T(8,128)S(1)} all-to-all(f32[32,16,128]{2,1,0:T(8,128)S(1)} %copy.153), channel_id=1, replica_groups=mesh['space'=32,'tm'=8] {'tm'}, dimensions={0} | all-to-all | bytes 524288 | tf_op jit(solution)/shard_map/all_to_all | solution.py:97
  (63 shorter events, 12.7 us)
Async XLA Ops:
  7.2 140.8 %all-reduce.7.cloned.1.call-start = ((), (), s32[]{:S(2)}) async-start(), calls=%async_computation.2 | async-start | bytes 524288 | tf_op jit(solution)/shard_map/psum | solution.py:11
  9.7 6.6 %collective-permute-start = (bf16[32,2,1024]{2,0,1:T(8,128)(2,1)S(1)}, bf16[32,2,1024]{2,0,1:T(8,128)(2,1)S(1)}, u32[]{:S(2)}, u32[]{:S(2)}) collective-permute-start(bf16[32,2,1024]{2,0,1:T(8,128)(2,1)S(1)} %get-tuple-element.18), channel_id=1, source_target_pairs={{0,8},{8,16},{16,24},{24,32},{32,40},{40,48},{48,56},{56,64},{64,7... | collective-permute-start | bytes 393224 | tf_op jit(solution)/shard_map/ppermute | solution.py:20
  9.8 6.5 %collective-permute-start.1 = (bf16[32,2,1024]{2,0,1:T(8,128)(2,1)S(1)}, bf16[32,2,1024]{2,0,1:T(8,128)(2,1)S(1)}, u32[]{:S(2)}, u32[]{:S(2)}) collective-permute-start(bf16[32,2,1024]{2,0,1:T(8,128)(2,1)S(1)} %get-tuple-element.19), channel_id=1, source_target_pairs={{8,0},{16,8},{24,16},{32,24},{40,32},{48,40},{56,48},{64,56},{72,6... | collective-permute-start | bytes 393224 | tf_op jit(solution)/shard_map/ppermute | solution.py:21
  19.5 5.1 %copy-start = (bf16[32,16,1024]{2,1,0:T(8,128)(2,1)}, bf16[32,16,1024]{2,1,0:T(8,128)(2,1)S(1)}, u32[]{:S(2)}) copy-start(bf16[32,16,1024]{2,1,0:T(8,128)(2,1)S(1)} %fusion.3) | copy-start | bytes 3145732
  79.7 181.1 %all-reduce.9.cloned.1.call-start = ((), (), s32[]{:S(2)}) async-start(), calls=%async_computation.3 | async-start | bytes 524288 | tf_op jit(solution)/shard_map/psum | solution.py:12
  261.7 29.5 %copy-start.1 = (f32[256,256]{0,1:T(8,128)S(1)}, f32[256,256]{0,1:T(8,128)}, u32[]{:S(2)}) copy-start(f32[256,256]{0,1:T(8,128)} %all-reduce.9.cloned.1.call-done) | copy-start | bytes 786436
Sparse Core Ops, SparseCore 0:
  79.8 68.0 all-reduce.6
  151.5 109.3 all-reduce.8
